TPU v7x, 32 devices: a whole 2x2x4 slice. The times are simulated.
32 devices in a mesh: dp: 8 (over y, x, core), mp: 4 (over z).
Axes of the slice: x: 2, y: 2, z: 4, core: 2. Of those that a mesh axis runs over, the one named last changes fastest.
Arguments:
- tokens: bfloat16 [16, 1024, 768], P('dp'), may hold values from -6 to 6
- lengths: int32 [16], P('dp'), may hold values from 256 to 1024, as said below
- qkv_weight: bfloat16 [3, 768, 768], P(None, None, 'mp'), may hold values from -0.5 to 0.5
- out_weight: bfloat16 [768, 768], P('mp'), may hold values from -0.3125 to 0.3125
- conv_taps: float32 [12, 33], P('mp'), may hold values from -0.36 to 0.36
- norm1_gain: float32 [768], replicated, may hold values from 0.1 to 1.9
- norm1_bias: float32 [768], replicated, may hold values from -0.5 to 0.5
- norm2_gain: float32 [768], replicated, may hold values from 0.1 to 1.9
- norm2_bias: float32 [768], replicated, may hold values from -0.5 to 0.5
- up_weight: bfloat16 [768, 3072], P(None, 'mp'), may hold values from -0.21875 to 0.21875
- down_weight: bfloat16 [3072, 768], P('mp'), may hold values from -0.109375 to 0.109375
- cotangent: bfloat16 [16, 1024, 768], P('dp'), may hold values from -6 to 6
Outputs:
- output: bfloat16 [16, 1024, 768], P('dp')
- input_grad: bfloat16 [16, 1024, 768], P('dp')
- qkv_grad: float32 [3, 768, 768], P(None, None, 'mp')
- out_grad: float32 [768, 768], P('mp')
- taps_grad: float32 [12, 33], P('mp')
- norm1_gain_grad: float32 [768], replicated
- norm1_bias_grad: float32 [768], replicated
- norm2_gain_grad: float32 [768], replicated
- norm2_bias_grad: float32 [768], replicated
- up_grad: float32 [768, 3072], P(None, 'mp')
- down_grad: float32 [3072, 768], P('mp')
Inputs may be any that keep to these rules, and one draw needn't show every extreme that they name: Each entry of lengths is the document's true length, and at least one document in every draw has length exactly 1024.
All inputs are finite; a program needn't handle non-finite values.
Results may differ from a plain program's by a relative error of at most 0.024.
The roundings to bfloat16 on the way count: a program that leaves them out, or rounds other values in their place, can miss the bound.
Values may be sent and summed in bfloat16 or wider, within the bound.
A program may use at most 256 MiB of HBM per device.

v0:
```python
import jax
import jax.numpy as jnp
from jax import lax
from jax.sharding import PartitionSpec as P

HEAD_DIM = 64
LANDMARKS = 64
KSIZE = 33
NS_ITERS = 6
EPSILON = 1e-05
FULL_PRECISION = lax.Precision.HIGHEST


def layer_norm(values, gain_vec, shift_vec):
    average = jnp.mean(values, axis=-1, keepdims=True)
    centered = values - average
    variance = jnp.mean(centered * centered, axis=-1, keepdims=True)
    return centered * lax.rsqrt(variance + EPSILON) * gain_vec + shift_vec


def newton_schulz(kernel):
    identity_m = jnp.eye(kernel.shape[-1], dtype=kernel.dtype)
    total_sq = jnp.sum(kernel * kernel, axis=(1, 2), keepdims=True)
    kernel_inverse = jnp.swapaxes(kernel, 1, 2) / total_sq
    for sweep_no in range(NS_ITERS):
        product = jnp.einsum("hij,hjk->hik", kernel, kernel_inverse, precision=FULL_PRECISION)
        inner_term = 7.0 * identity_m - product
        inner_term = 15.0 * identity_m - jnp.einsum(
            "hij,hjk->hik", product, inner_term, precision=FULL_PRECISION
        )
        inner_term = 13.0 * identity_m - jnp.einsum(
            "hij,hjk->hik", product, inner_term, precision=FULL_PRECISION
        )
        kernel_inverse = 0.25 * jnp.einsum(
            "hij,hjk->hik", kernel_inverse, inner_term, precision=FULL_PRECISION
        )
    return kernel_inverse


def pinv_from(landmark_queries, landmark_keys):
    scores_scale_factor = HEAD_DIM ** (-0.5)
    second_scores = (
        jnp.einsum("ble,gle->lbg", landmark_queries, landmark_keys, precision=FULL_PRECISION)
        * scores_scale_factor
    )
    return newton_schulz(jax.nn.softmax(second_scores, axis=-1))


def depthwise(values, tap_weights):
    half_span = (KSIZE - 1) // 2
    seq_len = values.shape[0]
    padded = jnp.pad(values, ((half_span, half_span), (0, 0), (0, 0)))
    running = jnp.zeros_like(values)
    for offset in range(KSIZE):
        running = (
            running + padded[offset : offset + seq_len] * tap_weights[:, offset][None, :, None]
        )
    return running


def gelu_exact(values):
    return jax.nn.gelu(values, approximate=False)


def landmark_table(length, seq_len):
    places = jnp.arange(seq_len, dtype=jnp.int32)
    live_flag = places < length
    segment = places * LANDMARKS // length
    segment_membership = (
        (segment[None, :] == jnp.arange(LANDMARKS, dtype=jnp.int32)[:, None]) & live_flag[None, :]
    ).astype(jnp.float32)
    landmark_counts = jnp.sum(segment_membership, axis=1)
    return (segment_membership, landmark_counts, live_flag)


def masked_scores(landmark_queries, key_matrix, live_flag):
    scores_scale_factor = HEAD_DIM ** (-0.5)
    third_scores = (
        jnp.einsum("xyk,pyk->yxp", landmark_queries, key_matrix, preferred_element_type=jnp.float32)
        * scores_scale_factor
    )
    return jnp.where(live_flag[None, None, :], third_scores, -1e30)


def attend_forward(query_matrix, key_matrix, value_matrix, length, tap_weights):
    scores_scale_factor = HEAD_DIM ** (-0.5)
    seq_len = query_matrix.shape[0]
    segment_membership, landmark_counts, live_flag = landmark_table(length, seq_len)
    live_f = live_flag.astype(jnp.float32)
    membership_batch = segment_membership.astype(jnp.bfloat16)
    landmark_queries = (
        jnp.einsum(
            "ov,vaf->oaf", membership_batch, query_matrix, preferred_element_type=jnp.float32
        )
        / landmark_counts[:, None, None]
    ).astype(jnp.bfloat16)
    landmark_keys = (
        jnp.einsum("ov,vaf->oaf", membership_batch, key_matrix, preferred_element_type=jnp.float32)
        / landmark_counts[:, None, None]
    ).astype(jnp.bfloat16)
    first_scores = (
        jnp.einsum("wxe,pxe->xwp", query_matrix, landmark_keys, preferred_element_type=jnp.float32)
        * scores_scale_factor
    )
    lse_one = jax.nn.logsumexp(first_scores, axis=-1)
    first_kernel = jnp.exp(first_scores - lse_one[..., None]).astype(jnp.bfloat16)
    kernel_inverse = pinv_from(
        landmark_queries.astype(jnp.float32), landmark_keys.astype(jnp.float32)
    )
    third_scores = masked_scores(landmark_queries, key_matrix, live_flag)
    lse_three = jax.nn.logsumexp(third_scores, axis=-1)
    third_kernel = jnp.exp(third_scores - lse_three[..., None]).astype(jnp.bfloat16)
    landmark_summary = jnp.einsum(
        "olp,pon->oln", third_kernel, value_matrix, preferred_element_type=jnp.float32
    )
    mixing_matrix = jnp.einsum(
        "lcb,lbf->lcf", kernel_inverse, landmark_summary, precision=FULL_PRECISION
    ).astype(jnp.bfloat16)
    landmark_approximation = jnp.einsum(
        "wpb,wbi->pwi", first_kernel, mixing_matrix, preferred_element_type=jnp.float32
    )
    masked_v = value_matrix.astype(jnp.float32) * live_f[:, None, None]
    local_term = depthwise(masked_v, tap_weights)
    context = ((landmark_approximation + local_term) * live_f[:, None, None]).astype(jnp.bfloat16)
    return (
        context,
        (
            landmark_queries,
            landmark_keys,
            lse_one,
            lse_three,
            kernel_inverse,
            landmark_summary,
            mixing_matrix,
        ),
    )


def attend_backward(
    query_matrix, key_matrix, value_matrix, length, tap_weights, kept_state, grad_context
):
    (
        landmark_queries,
        landmark_keys,
        lse_one,
        lse_three,
        kernel_inverse,
        landmark_summary,
        mixing_matrix,
    ) = kept_state
    scores_scale_factor = HEAD_DIM ** (-0.5)
    seq_len = query_matrix.shape[0]
    segment_membership, landmark_counts, live_flag = landmark_table(length, seq_len)
    live_f = live_flag.astype(jnp.float32)
    grad_local = grad_context.astype(jnp.float32) * live_f[:, None, None]
    local_branch_gradient = grad_local.astype(jnp.bfloat16)
    masked_v = value_matrix.astype(jnp.float32) * live_f[:, None, None]
    unused, conv_pull = jax.vjp(depthwise, masked_v, tap_weights)
    grad_masked, grad_taps = conv_pull(grad_local)
    first_scores = (
        jnp.einsum("wxe,pxe->xwp", query_matrix, landmark_keys, preferred_element_type=jnp.float32)
        * scores_scale_factor
    )
    first_kernel = jnp.exp(first_scores - lse_one[..., None])
    mixing_gradient = jnp.einsum(
        "paj,ape->pje",
        first_kernel.astype(jnp.bfloat16),
        local_branch_gradient,
        preferred_element_type=jnp.float32,
    )
    grad_kernel_one = jnp.einsum(
        "upn,pyn->puy", local_branch_gradient, mixing_matrix, preferred_element_type=jnp.float32
    )
    first_scores_gradient = (
        first_kernel
        * (grad_kernel_one - jnp.sum(grad_kernel_one * first_kernel, axis=-1, keepdims=True))
    ).astype(jnp.bfloat16)
    inverse_gradient = jnp.einsum(
        "xfe,xge->xfg", mixing_gradient, landmark_summary, precision=FULL_PRECISION
    )
    summary_gradient = jnp.einsum(
        "exa,exu->eau", kernel_inverse, mixing_gradient, precision=FULL_PRECISION
    ).astype(jnp.bfloat16)
    third_scores = masked_scores(landmark_queries, key_matrix, live_flag)
    third_kernel = jnp.exp(third_scores - lse_three[..., None])
    grad_kernel_three = jnp.einsum(
        "jbq,kjq->jbk", summary_gradient, value_matrix, preferred_element_type=jnp.float32
    )
    third_scores_gradient = (
        third_kernel
        * (grad_kernel_three - jnp.sum(grad_kernel_three * third_kernel, axis=-1, keepdims=True))
    ).astype(jnp.bfloat16)
    unused_inv, pinv_pull = jax.vjp(
        pinv_from, landmark_queries.astype(jnp.float32), landmark_keys.astype(jnp.float32)
    )
    landmark_query_gradient, landmark_key_gradient = pinv_pull(inverse_gradient)
    landmark_query_gradient = (
        landmark_query_gradient
        + jnp.einsum(
            "tni,itu->ntu", third_scores_gradient, key_matrix, preferred_element_type=jnp.float32
        )
        * scores_scale_factor
    )
    landmark_key_gradient = (
        landmark_key_gradient
        + jnp.einsum(
            "nxc,xnk->cnk", first_scores_gradient, query_matrix, preferred_element_type=jnp.float32
        )
        * scores_scale_factor
    )
    spread_q = jnp.einsum(
        "bq,brw->qrw",
        segment_membership,
        landmark_query_gradient / landmark_counts[:, None, None],
        precision=FULL_PRECISION,
    )
    spread_k = jnp.einsum(
        "bq,brw->qrw",
        segment_membership,
        landmark_key_gradient / landmark_counts[:, None, None],
        precision=FULL_PRECISION,
    )
    grad_query = (
        jnp.einsum(
            "nfc,cnk->fnk", first_scores_gradient, landmark_keys, preferred_element_type=jnp.float32
        )
        * scores_scale_factor
        + spread_q
    )
    grad_key = (
        jnp.einsum(
            "zpw,pzv->wzv",
            third_scores_gradient,
            landmark_queries,
            preferred_element_type=jnp.float32,
        )
        * scores_scale_factor
        + spread_k
    )
    grad_value = (
        jnp.einsum(
            "zrb,zrc->bzc",
            third_kernel.astype(jnp.bfloat16),
            summary_gradient,
            preferred_element_type=jnp.float32,
        )
        + grad_masked * live_f[:, None, None]
    )
    return (
        grad_query.astype(jnp.bfloat16),
        grad_key.astype(jnp.bfloat16),
        grad_value.astype(jnp.bfloat16),
        grad_taps,
    )


def body(
    tokens,
    lengths,
    qkv_weight,
    out_weight,
    conv_taps,
    norm1_gain,
    norm1_bias,
    norm2_gain,
    norm2_bias,
    up_weight,
    down_weight,
    cotangent,
):
    slot_count, seq_len, model_width = tokens.shape
    row_count = slot_count * seq_len
    local_heads = conv_taps.shape[0]
    local_width = local_heads * HEAD_DIM
    flat = tokens.reshape(row_count, model_width)
    places = jnp.arange(seq_len, dtype=jnp.int32)
    live_rows = (places[None, :] < lengths[:, None]).astype(jnp.float32).reshape(row_count)
    projected = jnp.einsum(
        "rd,tdc->trc", flat, qkv_weight, preferred_element_type=jnp.float32
    ).astype(jnp.bfloat16)
    per_head = projected.reshape(3, slot_count, seq_len, local_heads, HEAD_DIM)
    attend_all = jax.vmap(attend_forward, in_axes=(0, 0, 0, 0, None))
    context, kept_state = attend_all(per_head[0], per_head[1], per_head[2], lengths, conv_taps)
    context_flat = context.reshape(row_count, local_width)
    attn_part = jnp.einsum(
        "rc,cd->rd", context_flat, out_weight, preferred_element_type=jnp.float32
    )
    attn_out = lax.psum(attn_part.astype(jnp.bfloat16), "mp").astype(jnp.float32)
    mixed = flat.astype(jnp.float32) + attn_out
    normed, ln_one_pull = jax.vjp(layer_norm, mixed, norm1_gain, norm1_bias)
    normed_b = normed.astype(jnp.bfloat16)
    hidden_pre = jnp.einsum("rd,df->rf", normed_b, up_weight, preferred_element_type=jnp.float32)
    activated, gelu_pull = jax.vjp(gelu_exact, hidden_pre)
    activated_b = activated.astype(jnp.bfloat16)
    branch_part = jnp.einsum(
        "rf,fd->rd", activated_b, down_weight, preferred_element_type=jnp.float32
    )
    branch = lax.psum(branch_part.astype(jnp.bfloat16), "mp").astype(jnp.float32)
    final_norm, ln_two_pull = jax.vjp(layer_norm, normed + branch, norm2_gain, norm2_bias)
    output = (
        (final_norm * live_rows[:, None])
        .astype(jnp.bfloat16)
        .reshape(slot_count, seq_len, model_width)
    )
    grad_out = cotangent.reshape(row_count, model_width).astype(jnp.float32) * live_rows[:, None]
    grad_resid, grad_gain_two, grad_bias_two = ln_two_pull(grad_out)
    grad_branch_b = grad_resid.astype(jnp.bfloat16)
    grad_down = jnp.einsum(
        "rf,rd->fd", activated_b, grad_branch_b, preferred_element_type=jnp.float32
    )
    grad_act = jnp.einsum(
        "rd,fd->rf", grad_branch_b, down_weight, preferred_element_type=jnp.float32
    )
    grad_pre = gelu_pull(grad_act)[0].astype(jnp.bfloat16)
    grad_up = jnp.einsum("rd,rf->df", normed_b, grad_pre, preferred_element_type=jnp.float32)
    normed_part = jnp.einsum("rf,df->rd", grad_pre, up_weight, preferred_element_type=jnp.float32)
    grad_normed = grad_resid + lax.psum(normed_part.astype(jnp.bfloat16), "mp").astype(jnp.float32)
    grad_mixed, grad_gain_one, grad_bias_one = ln_one_pull(grad_normed)
    small_grads = jnp.stack([grad_gain_one, grad_bias_one, grad_gain_two, grad_bias_two])
    grad_attn_b = grad_mixed.astype(jnp.bfloat16)
    grad_outw = jnp.einsum(
        "rc,rd->cd", context_flat, grad_attn_b, preferred_element_type=jnp.float32
    )
    grad_context = jnp.einsum(
        "rd,cd->rc", grad_attn_b, out_weight, preferred_element_type=jnp.float32
    ).astype(jnp.bfloat16)
    grad_context = grad_context.reshape(slot_count, seq_len, local_heads, HEAD_DIM)
    back_all = jax.vmap(attend_backward, in_axes=(0, 0, 0, 0, None, 0, 0))
    grad_query, grad_key, grad_value, grad_taps = back_all(
        per_head[0], per_head[1], per_head[2], lengths, conv_taps, kept_state, grad_context
    )
    grad_proj = jnp.stack([grad_query, grad_key, grad_value]).reshape(3, row_count, local_width)
    grad_qkv = jnp.einsum("rd,trc->tdc", flat, grad_proj, preferred_element_type=jnp.float32)
    input_part = jnp.einsum(
        "trc,tdc->rd", grad_proj, qkv_weight, preferred_element_type=jnp.float32
    )
    input_grad = (
        grad_mixed + lax.psum(input_part.astype(jnp.bfloat16), "mp").astype(jnp.float32)
    ).astype(jnp.bfloat16)
    input_grad = input_grad.reshape(slot_count, seq_len, model_width)
    taps_pad = jnp.pad(jnp.sum(grad_taps, axis=0), ((0, 0), (0, model_width - KSIZE)))
    shares = (
        lax.psum_scatter(grad_qkv, "dp", scatter_dimension=1, tiled=True),
        lax.psum_scatter(grad_outw, "dp", scatter_dimension=1, tiled=True),
        lax.psum_scatter(taps_pad, "dp", scatter_dimension=1, tiled=True),
        lax.psum_scatter(grad_up, "dp", scatter_dimension=0, tiled=True),
        lax.psum_scatter(grad_down, "dp", scatter_dimension=1, tiled=True),
        lax.psum_scatter(small_grads, "dp", scatter_dimension=1, tiled=True),
    )
    sync_qkv, sync_outw, sync_taps, sync_up, sync_down, sync_small = (
        lax.all_gather(shares[0].astype(jnp.bfloat16), "dp", axis=1, tiled=True).astype(
            jnp.float32
        ),
        lax.all_gather(shares[1].astype(jnp.bfloat16), "dp", axis=1, tiled=True).astype(
            jnp.float32
        ),
        lax.all_gather(shares[2].astype(jnp.bfloat16), "dp", axis=1, tiled=True).astype(
            jnp.float32
        ),
        lax.all_gather(shares[3].astype(jnp.bfloat16), "dp", axis=0, tiled=True).astype(
            jnp.float32
        ),
        lax.all_gather(shares[4].astype(jnp.bfloat16), "dp", axis=1, tiled=True).astype(
            jnp.float32
        ),
        lax.all_gather(shares[5].astype(jnp.bfloat16), "dp", axis=1, tiled=True).astype(
            jnp.float32
        ),
    )
    return (
        output,
        input_grad,
        sync_qkv,
        sync_outw,
        sync_taps[:, :KSIZE],
        sync_small[0],
        sync_small[1],
        sync_small[2],
        sync_small[3],
        sync_up,
        sync_down,
    )


def solution(mesh):
    return jax.shard_map(
        body,
        mesh=mesh,
        in_specs=(
            P("dp", None, None),
            P("dp"),
            P(None, None, "mp"),
            P("mp", None),
            P("mp", None),
            P(),
            P(),
            P(),
            P(),
            P(None, "mp"),
            P("mp", None),
            P("dp", None, None),
        ),
        out_specs=(
            P("dp", None, None),
            P("dp", None, None),
            P(None, None, "mp"),
            P("mp", None),
            P("mp", None),
            P(),
            P(),
            P(),
            P(),
            P(None, "mp"),
            P("mp", None),
        ),
        check_vma=False,
    )
```

profile of v0, /device:TPU:0, one launch (start us, length us, event | category | flops | bytes accessed | tf_op | source)
XLA Modules:
  0.0 951.2 jit_solution(3927351751233964447)
XLA Ops:
  7.8 2.2 slice_reduce_fusion.35
  10.0 2.5 slice_reduce_fusion.36
  16.2 4.2 fusion.10
  21.5 1.5 squeeze.15
  28.3 2.2 fusion.132
  30.5 3.1 squeeze.16
  51.4 36.9 %fusion.18 = bf16[2,1024,3,64]{1,3,2,0:T(8,128)(2,1)} fusion(f32[2,1024,3,64]{1,3,2,0:T(8,128)} %convert_multiply_fusion, bf16[2,3,64,64]{3,2,1,0:T(8,128)(2,1)} %convolution_convert_fusion.6, f32[3]{0:T(128)} %get-tuple-element.140, f32[3]{0:T(128)} %get-tuple-element.141, f32[3]{0:T(128)} %get-tuple-element.110, f32[3]{0:T(128)} %get-tuple-element.111, ...), kind=kOutput, calls=%fused_computation.63 | convolution fusion | flops 77856768 | bytes 4014476 | tf_op jit(solution)/shard_map/vmap(wpb,wbi->pwi)/dot_general | solution.py:119
  88.2 2.0 copy.226
  91.3 2.7 convolution_convert_fusion.2
  94.1 123.9 %all-reduce.73.cloned.1.call-done = bf16[2048,768]{1,0:T(8,128)(2,1)} async-done(((bf16[2048,768]{1,0:T(8,128)(2,1)}), bf16[2048,768]{1,0:T(8,128)(2,1)}) %all-reduce.73.cloned.1.call-update) | async-done | bytes 3145744 | tf_op jit(solution)/shard_map/psum | solution.py:288
  218.0 3.9 fusion.7
  222.7 2.0 multiply_reduce_fusion.6
  224.8 17.7 %multiply_convert_fusion.1 = (bf16[2048,768]{1,0:T(8,128)(2,1)S(1)}, f32[2048,768]{1,0:T(8,128)}, f32[2048,768]{1,0:T(8,128)}) fusion(bf16[768,768]{1,0:T(8,128)(2,1)S(1)} %copy-done, f32[2048,768]{1,0:T(8,128)S(1)} %get-tuple-element.151, f32[768]{0:T(1024)S(1)} %copy-done.118, f32[768]{0:T(1024)S(1)} %copy-done.106, f32[2048]{0:T(1024)S(1)} %fusion.107), kind=kOutput, calls=%fused_computation.17 | convolution fusion | flops 2524446720 | bytes 23214080 | tf_op jit(solution)/shard_map/rd,df->rf/dot_general | solution.py:292
  242.5 1.8 copy-done.162
  244.3 3.9 convolution_convert_fusion.1
  248.9 119.6 %all-reduce.75.cloned.1.call-done = bf16[2048,768]{1,0:T(8,128)(2,1)} async-done(((bf16[2048,768]{1,0:T(8,128)(2,1)}), bf16[2048,768]{1,0:T(8,128)(2,1)}) %all-reduce.75.cloned.1.call-update) | async-done | bytes 3145744 | tf_op jit(solution)/shard_map/psum | solution.py:298
  368.5 4.6 fusion.126
  375.0 2.6 multiply_reduce_fusion.1
  377.7 4.9 fusion.125
  382.6 4.6 add_convert_fusion.1
  387.3 1.7 copy-done.160
  389.0 4.0 convolution_convert_fusion
  393.4 7.9 fusion.112
  401.5 2.7 multiply_reduce_fusion
  405.4 7.1 fusion.114
  412.5 100.7 %all-reduce.77.cloned.1.call-done = bf16[2048,768]{1,0:T(8,128)(2,1)} async-done(((bf16[2048,768]{1,0:T(8,128)(2,1)}), bf16[2048,768]{1,0:T(8,128)(2,1)}) %all-reduce.77.cloned.1.call-update) | async-done | bytes 3145744 | tf_op jit(solution)/shard_map/psum | solution.py:317
  513.2 7.0 multiply_reduce_fusion.2
  520.3 6.7 fusion.124
  527.0 2.6 copy-done.6
  529.6 2.5 fusion.11
  532.1 2.8 reshape.458
  535.0 2.2 fusion.58
  562.9 7.8 multiply_reduce_fusion.39
  570.7 8.4 multiply_reduce_fusion.38
  581.5 2.2 multiply_reduce_fusion.40
  586.4 1.9 multiply_reduce_fusion.41
  588.4 2.6 convolution_bitcast_fusion.1
  592.9 1.9 fusion.56
  594.9 2.4 multiply_convert_fusion.3
  599.9 8.6 broadcast_multiply_fusion.1
  608.6 1.6 convert_element_type.249
  611.1 9.5 %broadcast_multiply_fusion = (f32[2,1024,3,64]{1,3,2,0:T(8,128)}, f32[2,1024,3,64]{1,3,2,0:T(8,128)}, f32[2,1024,3,64]{1,3,2,0:T(8,128)}, f32[2,1024,3,64]{1,3,2...) fusion(f32[3]{0:T(128)S(1)} %copy-done.142, ...), kind=kLoop, calls=%fused_computation.230 | loop fusion | flops 7077888 | bytes 28319948 | tf_op jit(solution)/shard_map/vmap(transpose(jvp()))/mul | solution.py:56
  620.7 20.5 %pad_add_fusion = f32[2,1056,3,64]{1,3,2,0:T(8,128)} fusion(f32[2,1024,3,64]{1,3,2,0:T(8,128)} %get-tuple-element.160, f32[2,1024,3,64]{1,3,2,0:T(8,128)} %get-tuple-element.161, f32[2,1024,3,64]{1,3,2,0:T(8,128)} %get-tuple-element.162, f32[2,1024,3,64]{1,3,2,0:T(8,128)} %get-tuple-element.163, f32[2,1024,3,64]{1,3,2,0:T(8,128)} %get-tuple-element.164, ...), kind=kLoop, calls=%fused_computation.47 | loop fusion | flops 10543104 | bytes 44089344 | tf_op jit(solution)/shard_map/vmap(transpose(jvp()))/add_any | solution.py:56
  641.3 1.6 convert_element_type.247
  645.4 1.6 fusion.15
  647.8 1.5 stack.20
  649.3 7.5 fusion.14
  660.8 2.0 convolution_bitcast_fusion
  662.8 2.7 copy.302
  665.5 4.8 reshape.471
  671.5 4.0 bitcast_convert_fusion
  676.4 8.8 all-gather
  686.7 8.8 all-gather.1
  696.3 21.4 %reduce-scatter.21.cloned.1.call-done = f32[96,192]{1,0:T(8,128)} async-done(((f32[768,192]{1,0:T(8,128)}), f32[96,192]{1,0:T(8,128)}) %reduce-scatter.21.cloned.1.call-update) | async-done | bytes 73744
  718.7 9.5 %all_gather.19 = bf16[192,768]{0,1:T(8,128)(2,1)S(1)} all-gather(bf16[192,96]{0,1:T(8,128)(2,1)S(1)} %copy.262), channel_id=1, replica_groups=mesh['dp'=8,'mp'=4] {'dp'}, dimensions={1}, use_global_device_ids=true | all-gather | bytes 331776 | tf_op jit(solution)/shard_map/all_gather | solution.py:354
  729.2 14.4 %all-gather.7.cloned.1.call-done = bf16[768,768]{0,1:T(8,128)(2,1)} async-done(((bf16[768,96]{0,1:T(8,128)(2,1)}), bf16[768,768]{0,1:T(8,128)(2,1)}) %all-gather.7.cloned.1.call-update) | async-done | bytes 1179664 | tf_op jit(solution)/shard_map/all_gather | solution.py:363
  743.6 2.7 copy.268
  746.3 23.7 %all-gather.5.cloned.1.call-done = bf16[768,768]{1,0:T(8,128)(2,1)} async-done(((bf16[96,768]{1,0:T(8,128)(2,1)}), bf16[768,768]{1,0:T(8,128)(2,1)}) %all-gather.5.cloned.1.call-update) | async-done | bytes 1179664 | tf_op jit(solution)/shard_map/all_gather | solution.py:360
  770.0 2.8 convert_element_type.248
  772.9 40.9 %reduce-scatter.19.cloned.1.call-done = f32[96,576]{1,0:T(8,128)} async-done(((f32[768,576]{1,0:T(8,128)}), f32[96,576]{1,0:T(8,128)}) %reduce-scatter.19.cloned.1.call-update) | async-done | bytes 221200
  815.2 12.1 %all_gather.18 = bf16[3,768,192]{2,0,1:T(4,128)(2,1)S(1)} all-gather(bf16[3,96,192]{2,0,1:T(4,128)(2,1)S(1)} %copy.261), channel_id=1, replica_groups=mesh['dp'=8,'mp'=4] {'dp'}, dimensions={1}, use_global_device_ids=true | all-gather | bytes 995328 | tf_op jit(solution)/shard_map/all_gather | solution.py:351
  827.3 2.2 copy.266
  829.5 108.3 %all-reduce.79.cloned.1.call-done = bf16[2048,768]{1,0:T(8,128)(2,1)} async-done(((bf16[2048,768]{1,0:T(8,128)(2,1)}), bf16[2048,768]{1,0:T(8,128)(2,1)}) %all-reduce.79.cloned.1.call-update) | async-done | bytes 3145744 | tf_op jit(solution)/shard_map/psum | solution.py:338
  937.8 6.3 add_convert_fusion
  (518 shorter events, 84.2 us)
Async XLA Ops:
  7.2 217.6 %copy-start = (bf16[768,768]{1,0:T(8,128)(2,1)S(1)}, bf16[768,768]{1,0:T(8,128)(2,1)}, u32[]{:S(2)}) copy-start(bf16[768,768]{1,0:T(8,128)(2,1)} %param.23) | copy-start | bytes 3538948
  7.2 210.8 %all-reduce.73.cloned.1.call-start = ((), (), s32[]{:S(2)}) async-start(), calls=%async_computation.6 | async-start | bytes 6291456 | tf_op jit(solution)/shard_map/psum | solution.py:288
  15.0 11.0 %copy-start.99 = (pred[2,1024]{1,0:T(4,128)(4,1)}, pred[2,1024]{1,0:T(4,128)(4,1)S(1)}, u32[]{:S(2)}) copy-start(pred[2,1024]{1,0:T(4,128)(4,1)S(1)} %get-tuple-element.191) | copy-start | bytes 6148
  23.5 4.8 copy-start.36
  25.5 2.8 copy-start.85
  26.7 3.8 copy-start.83
  27.3 18.4 %copy-start.104 = (f32[2,3,64]{2,1,0:T(4,128)}, f32[2,3,64]{2,1,0:T(4,128)S(1)}, u32[]{:S(2)}) copy-start(f32[2,3,64]{2,1,0:T(4,128)S(1)} %get-tuple-element.194) | copy-start | bytes 4612
  27.3 20.8 %copy-start.3 = (f32[2,3,64,1024]{3,2,1,0:T(8,128)}, f32[2,3,64,1024]{3,2,1,0:T(8,128)S(1)}, u32[]{:S(2)}) copy-start(f32[2,3,64,1024]{3,2,1,0:T(8,128)S(1)} %get-tuple-element.195) | copy-start | bytes 4718596
  34.7 9.3 copy-start.17
  35.4 2.6 copy-start.19
  37.7 2.6 copy-start.21
  45.7 4.7 copy-start.77
  48.6 2.7 copy-start.9
  88.2 3.1 copy-start.82
  94.1 274.4 %all-reduce.75.cloned.1.call-start = ((), (), s32[]{:S(2)}) async-start(), calls=%async_computation.7 | async-start | bytes 6291456 | tf_op jit(solution)/shard_map/psum | solution.py:298
  218.0 3.9 copy-start.14
  218.0 4.7 copy-start.16
  224.7 17.8 %copy-start.2 = (f32[2048,768]{1,0:T(8,128)}, f32[2048,768]{1,0:T(8,128)S(1)}, u32[]{:S(2)}) copy-start(f32[2048,768]{1,0:T(8,128)S(1)} %get-tuple-element.151) | copy-start | bytes 18874372
  224.8 19.5 %copy-start.155 = (bf16[768,768]{1,0:T(8,128)(2,1)S(1)}, bf16[768,768]{1,0:T(8,128)(2,1)}, u32[]{:S(2)}) copy-start(bf16[768,768]{1,0:T(8,128)(2,1)} %param.24) | copy-start | bytes 3538948
  248.2 265.0 %all-reduce.77.cloned.1.call-start = ((), (), s32[]{:S(2)}) async-start(), calls=%async_computation.8 | async-start | bytes 6291456 | tf_op jit(solution)/shard_map/psum | solution.py:317
  375.0 2.7 copy-start.117
  375.0 7.6 slice-start.2
  375.0 7.6 slice-start.4
  377.7 4.9 slice-start.3
  377.7 4.9 slice-start.5
  382.6 4.7 copy-start.7
  393.0 215.6 %reduce-scatter.17.cloned.1.call-start = ((), (), s32[]{:S(2)}) async-start(), calls=%async_computation.12 | async-start | bytes 2654208 | tf_op jit(solution)/shard_map/reduce_scatter | solution.py:347
  401.4 3.4 copy-start.114
  401.4 239.8 %reduce-scatter.15.cloned.1.call-start = ((), (), s32[]{:S(2)}) async-start(), calls=%async_computation.10 | async-start | bytes 2654208 | tf_op jit(solution)/shard_map/reduce_scatter | solution.py:346
  401.4 3.9 copy-start.161
  412.5 263.1 %reduce-scatter.23.cloned.1.call-start = ((), (), s32[]{:S(2)}) async-start(), calls=%async_computation.16 | async-start | bytes 442368
  513.2 7.0 copy-start.13
  527.0 2.7 copy-start.6
  527.0 5.1 copy-start.101
  532.1 2.8 copy-start.91
  535.0 2.7 copy-start.74
  535.0 3.2 copy-start.49
  562.9 7.8 copy-start.151
  570.7 9.3 copy-start.66
  579.2 4.9 copy-start.41
  581.5 6.9 slice-start
  583.7 4.6 slice-start.1
  588.4 2.7 copy-start.86
  588.4 2.7 copy-start.115
  588.4 2.7 copy-start.153
  588.4 2.7 copy-start.158
  591.0 94.8 %reduce-scatter.25.cloned.1.call-start = ((), (), s32[]{:S(2)}) async-start(), calls=%async_computation.17 | async-start | bytes 442368
  592.8 124.8 %reduce-scatter.21.cloned.1.call-start = ((), (), s32[]{:S(2)}) async-start(), calls=%async_computation.15 | async-start | bytes 884736
  594.8 148.8 %all-gather.7.cloned.1.call-start = ((), (), s32[]{:S(2)}) async-start(), calls=%async_computation.13 | async-start | bytes 1327104 | tf_op jit(solution)/shard_map/all_gather | solution.py:363
  599.8 10.7 %copy-start.84 = (bf16[2,64,3,64]{3,1,2,0:T(8,128)(2,1)S(1)}, bf16[2,64,3,64]{3,1,2,0:T(8,128)(2,1)}, u32[]{:S(2)}) copy-start(bf16[2,64,3,64]{3,1,2,0:T(8,128)(2,1)} %copy-done.83) | copy-start | bytes 147460
  599.8 10.7 %copy-start.116 = (f32[2,3,64]{2,1,0:T(4,128)S(1)}, f32[2,3,64]{2,1,0:T(4,128)}, u32[]{:S(2)}) copy-start(f32[2,3,64]{2,1,0:T(4,128)} %neg.102) | copy-start | bytes 4612
  599.8 10.7 %copy-start.154 = (f32[2,64]{1,0:T(2,128)S(1)}, f32[2,64]{1,0:T(2,128)}, u32[]{:S(2)}) copy-start(f32[2,64]{1,0:T(2,128)} %copy-done.152) | copy-start | bytes 1540
  599.9 10.7 %copy-start.157 = (f32[2,64,3,64]{3,1,2,0:T(8,128)S(1)}, f32[2,64,3,64]{3,1,2,0:T(8,128)}, u32[]{:S(2)}) copy-start(f32[2,64,3,64]{3,1,2,0:T(8,128)} %fusion.40) | copy-start | bytes 294916
  599.9 10.7 %copy-start.159 = (f32[2,3,64,64]{2,3,1,0:T(8,128)S(1)}, f32[2,3,64,64]{2,3,1,0:T(8,128)}, u32[]{:S(2)}) copy-start(f32[2,3,64,64]{2,3,1,0:T(8,128)} %get-tuple-element.204) | copy-start | bytes 294916
  608.5 2.5 copy-start.137
  608.5 2.5 copy-start.138
  608.5 2.5 copy-start.139
  610.3 159.7 %all-gather.5.cloned.1.call-start = ((), (), s32[]{:S(2)}) async-start(), calls=%async_computation.11 | async-start | bytes 1327104 | tf_op jit(solution)/shard_map/all_gather | solution.py:360
  642.9 170.9 %reduce-scatter.19.cloned.1.call-start = ((), (), s32[]{:S(2)}) async-start(), calls=%async_computation.14 | async-start | bytes 2211840
  658.2 2.6 copy-start.15
  665.5 5.1 copy-start.96
  670.3 267.5 %all-reduce.79.cloned.1.call-start = ((), (), s32[]{:S(2)}) async-start(), calls=%async_computation.9 | async-start | bytes 6291456 | tf_op jit(solution)/shard_map/psum | solution.py:338
  827.3 110.5 %copy-start.103 = (f32[2048]{0:T(1024)S(1)}, f32[2048]{0:T(1024)}, u32[]{:S(2)}) copy-start(f32[2048]{0:T(1024)} %copy-done.101) | copy-start | bytes 24580
  937.8 6.3 copy-start.1
  (117 other events, 201.9 us)
Sparse Core Ops, SparseCore 0:
  94.2 123.7 all-reduce.72
  248.4 120.0 all-reduce.74
  393.1 120.0 all-reduce.76
  517.0 41.5 reduce-scatter.16
  562.7 42.4 reduce-scatter.14
  608.7 33.8 reduce-scatter.22
  645.6 33.7 reduce-scatter.24
  682.6 34.9 reduce-scatter.20
  719.5 24.0 all-gather.6
  745.9 24.0 all-gather.4
  773.4 40.3 reduce-scatter.18
  816.7 121.0 all-reduce.78
where the time goes:
time: 957 us; the launch traced here: 951 us
  waiting for transfers between devices  553 us (58%)
  matrix products  160 us (17%)
  other arithmetic  116 us (12%)
  local copies, waits for them, and re-layouts  63.3 us (7%)
  blocking collectives  39.2 us (4%)
  between operations  17.5 us (2%)
    psum x1, waiting for transfers between devices, body(): lax.psum(attn_part.astype(jnp.bfloat16), 'mp').astype(jnp.float32)  124 us
    psum x1, waiting for transfers between devices, body(): lax.psum(branch_part.astype(jnp.bfloat16), 'mp').astype(jnp.float32)  120 us
    psum x1, waiting for transfers between devices, body(): lax.psum(input_part.astype(jnp.bfloat16), 'mp').astype(jnp.float32)  108 us
    psum x1, waiting for transfers between devices, body(): lax.psum(normed_part.astype(jnp.bfloat16), 'mp').astype(jnp.float32)  101 us
    unnamed x16, waiting for transfers between devices  62.5 us
    unnamed x355, local copies, waits for them, and re-layouts  39 us
    dot_general x1, matrix products, attend_forward(): jnp.einsum('wpb,wbi->pwi', first_kernel, mixing_matrix, preferred_element...  36.9 us
    all_gather x1, waiting for transfers between devices, body(): lax.all_gather(shares[3].astype(jnp.bfloat16), 'dp', axis=0, tiled=True)  23.7 us
  transfers between devices with their start and end apart: 12, of which 8 were waited for; matrix products, arithmetic and copies ran while one was open for 19% of the time, Pallas kernels for 0%

commit v1 on v0

--- a/solution.py
+++ b/solution.py
@@ -335,7 +335,8 @@
         "trc,tdc->rd", grad_proj, qkv_weight, preferred_element_type=jnp.float32
     )
     input_grad = (
-        grad_mixed + lax.psum(input_part.astype(jnp.bfloat16), "mp").astype(jnp.float32)
+        grad_mixed
+        + jnp.sum(lax.all_gather(input_part.astype(jnp.bfloat16), "mp"), axis=0).astype(jnp.float32)
     ).astype(jnp.bfloat16)
     input_grad = input_grad.reshape(slot_count, seq_len, model_width)
     taps_pad = jnp.pad(jnp.sum(grad_taps, axis=0), ((0, 0), (0, model_width - KSIZE)))

time: 957 us -> 1060 us (1.11)
  waiting for transfers between devices: 553 us -> 627 us
  matrix products: 160 us -> 177 us
    all_gather x0 -> x1, waiting for transfers between devices: none -> 205 us  [body(): lax.all_gather(input_part.astype(jnp.bfloat16), 'mp')]
    psum x1 -> x0, waiting for transfers between devices: 108 us -> none  [body(): lax.psum(input_part.astype(jnp.bfloat16), 'mp').astype(jnp.float32)]
    unnamed x16, waiting for transfers between devices: 62.5 us -> 41.2 us
    unnamed x355 -> x341, local copies, waits for them, and re-layouts: 39 us -> 35.4 us
  transfers between devices with their start and end apart: 12 -> 12, of which waited for: 8 -> 7; matrix products, arithmetic and copies ran while one was open for 19% -> 20% of each run, Pallas kernels for 0% -> 0%
where the time goes in v1:
time: 1060 us
  waiting for transfers between devices  627 us (59%)
  matrix products  177 us (17%)
  other arithmetic  125 us (12%)
  local copies, waits for them, and re-layouts  70.3 us (7%)
  blocking collectives  38.7 us (4%)
  between operations  17.3 us (2%)
    all_gather x1, waiting for transfers between devices, body(): lax.all_gather(input_part.astype(jnp.bfloat16), 'mp')  205 us
    psum x1, waiting for transfers between devices, body(): lax.psum(attn_part.astype(jnp.bfloat16), 'mp').astype(jnp.float32)  124 us
    psum x1, waiting for transfers between devices, body(): lax.psum(branch_part.astype(jnp.bfloat16), 'mp').astype(jnp.float32)  120 us
    psum x1, waiting for transfers between devices, body(): lax.psum(normed_part.astype(jnp.bfloat16), 'mp').astype(jnp.float32)  99.8 us
    unnamed x16, waiting for transfers between devices  41.2 us
    dot_general x1, matrix products, attend_forward(): jnp.einsum('wpb,wbi->pwi', first_kernel, mixing_matrix, preferred_element...  37.5 us
    unnamed x341, local copies, waits for them, and re-layouts  35.4 us
    all_gather x1, waiting for transfers between devices, body(): lax.all_gather(shares[3].astype(jnp.bfloat16), 'dp', axis=0, tiled=True)  23.1 us
  transfers between devices with their start and end apart: 12, of which 7 were waited for; matrix products, arithmetic and copies ran while one was open for 20% of the time, Pallas kernels for 0%

profile of v1, /device:TPU:0, one launch (start us, length us, event | category | flops | bytes accessed | tf_op | source)
XLA Modules:
  0.0 1056.1 jit_solution(5863120822550070500)
XLA Ops:
  7.3 2.2 slice_reduce_fusion.35
  9.4 2.5 slice_reduce_fusion.36
  13.9 4.2 fusion.10
  25.9 2.3 fusion.132
  28.1 3.4 squeeze.16
  49.8 37.5 %fusion.18 = bf16[2,1024,3,64]{1,3,2,0:T(8,128)(2,1)} fusion(f32[2,1024,3,64]{1,3,2,0:T(8,128)} %convert_multiply_fusion, bf16[2,3,64,64]{3,2,1,0:T(8,128)(2,1)} %convolution_convert_fusion.6, f32[3]{0:T(128)} %get-tuple-element.140, f32[3]{0:T(128)} %get-tuple-element.141, f32[3]{0:T(128)} %get-tuple-element.110, f32[3]{0:T(128)} %get-tuple-element.111, ...), kind=kOutput, calls=%fused_computation.63 | convolution fusion | flops 77856768 | bytes 4014476 | tf_op jit(solution)/shard_map/vmap(wpb,wbi->pwi)/dot_general | solution.py:119
  87.3 2.0 copy.226
  90.3 2.7 convolution_convert_fusion.2
  93.1 123.9 %all-reduce.72.cloned.1.call-done = bf16[2048,768]{1,0:T(8,128)(2,1)} async-done(((bf16[2048,768]{1,0:T(8,128)(2,1)}), bf16[2048,768]{1,0:T(8,128)(2,1)}) %all-reduce.72.cloned.1.call-update) | async-done | bytes 3145744 | tf_op jit(solution)/shard_map/psum | solution.py:288
  217.0 3.9 fusion.7
  221.7 1.8 multiply_reduce_fusion.6
  223.6 17.7 %multiply_convert_fusion.1 = (bf16[2048,768]{1,0:T(8,128)(2,1)S(1)}, f32[2048,768]{1,0:T(8,128)}, f32[2048,768]{1,0:T(8,128)}) fusion(bf16[768,768]{1,0:T(8,128)(2,1)S(1)} %copy-done, f32[2048,768]{1,0:T(8,128)S(1)} %get-tuple-element.151, f32[768]{0:T(1024)S(1)} %copy-done.114, f32[768]{0:T(1024)S(1)} %copy-done.102, f32[2048]{0:T(1024)S(1)} %fusion.107), kind=kOutput, calls=%fused_computation.17 | convolution fusion | flops 2524446720 | bytes 23214080 | tf_op jit(solution)/shard_map/rd,df->rf/dot_general | solution.py:292
  241.3 1.8 copy-done.157
  243.1 3.9 convolution_convert_fusion.1
  247.7 119.6 %all-reduce.74.cloned.1.call-done = bf16[2048,768]{1,0:T(8,128)(2,1)} async-done(((bf16[2048,768]{1,0:T(8,128)(2,1)}), bf16[2048,768]{1,0:T(8,128)(2,1)}) %all-reduce.74.cloned.1.call-update) | async-done | bytes 3145744 | tf_op jit(solution)/shard_map/psum | solution.py:298
  367.3 4.8 fusion.126
  374.0 2.6 multiply_reduce_fusion.1
  376.7 4.9 fusion.125
  381.6 5.4 add_convert_fusion.1
  387.0 6.2 convolution_convert_fusion
  393.3 7.9 fusion.112
  401.5 2.7 multiply_reduce_fusion
  406.6 7.0 fusion.114
  413.7 99.8 %all-reduce.76.cloned.1.call-done = bf16[2048,768]{1,0:T(8,128)(2,1)} async-done(((bf16[2048,768]{1,0:T(8,128)(2,1)}), bf16[2048,768]{1,0:T(8,128)(2,1)}) %all-reduce.76.cloned.1.call-update) | async-done | bytes 3145744 | tf_op jit(solution)/shard_map/psum | solution.py:317
  513.5 7.6 multiply_reduce_fusion.2
  521.1 8.2 fusion.124
  530.0 5.2 fusion.11
  535.2 3.0 reshape.458
  538.3 2.2 fusion.58
  566.3 7.8 multiply_reduce_fusion.39
  574.1 8.2 multiply_reduce_fusion.38
  584.6 1.8 multiply_reduce_fusion.40
  589.3 1.9 multiply_reduce_fusion.41
  591.3 5.5 convolution_bitcast_fusion.1
  596.9 2.1 fusion.38
  600.6 1.7 copy.252
  602.4 2.9 fusion.56
  605.4 2.4 multiply_convert_fusion.3
  610.5 8.6 broadcast_multiply_fusion.1
  621.5 2.0 fusion.36
  624.6 9.6 broadcast_multiply_fusion
  634.2 20.6 %pad_add_fusion = f32[2,1056,3,64]{1,3,2,0:T(8,128)} fusion(f32[2,1024,3,64]{1,3,2,0:T(8,128)} %get-tuple-element.160, f32[2,1024,3,64]{1,3,2,0:T(8,128)} %get-tuple-element.161, f32[2,1024,3,64]{1,3,2,0:T(8,128)} %get-tuple-element.162, f32[2,1024,3,64]{1,3,2,0:T(8,128)} %get-tuple-element.163, f32[2,1024,3,64]{1,3,2,0:T(8,128)} %get-tuple-element.164, ...), kind=kLoop, calls=%fused_computation.47 | loop fusion | flops 10543104 | bytes 44089344 | tf_op jit(solution)/shard_map/vmap(transpose(jvp()))/add_any | solution.py:56
  657.3 2.8 copy.253
  660.2 3.4 stack.19
  665.1 1.7 copy.258
  666.8 3.2 stack.20
  670.1 6.9 fusion.14
  681.0 2.0 convolution_bitcast_fusion
  683.0 2.7 copy.302
  685.7 4.6 reshape.472
  691.5 6.0 bitcast_convert_fusion
  698.5 9.0 all-gather.1
  709.0 8.8 all-gather.2
  719.6 8.9 all_gather.27
  729.5 14.4 %all-gather.9.cloned.1.call-done = bf16[768,768]{0,1:T(8,128)(2,1)} async-done(((bf16[768,96]{0,1:T(8,128)(2,1)}), bf16[768,768]{0,1:T(8,128)(2,1)}) %all-gather.9.cloned.1.call-update) | async-done | bytes 1179664 | tf_op jit(solution)/shard_map/all_gather | solution.py:364
  743.9 2.7 copy.268
  746.6 23.1 %all-gather.7.cloned.1.call-done = bf16[768,768]{1,0:T(8,128)(2,1)} async-done(((bf16[96,768]{1,0:T(8,128)(2,1)}), bf16[768,768]{1,0:T(8,128)(2,1)}) %all-gather.7.cloned.1.call-update) | async-done | bytes 1179664 | tf_op jit(solution)/shard_map/all_gather | solution.py:361
  769.7 2.8 convert_element_type.250
  772.5 40.9 %reduce-scatter.19.cloned.1.call-done = f32[96,576]{1,0:T(8,128)} async-done(((f32[768,576]{1,0:T(8,128)}), f32[96,576]{1,0:T(8,128)}) %reduce-scatter.19.cloned.1.call-update) | async-done | bytes 221200
  814.9 12.1 %all_gather.26 = bf16[3,768,192]{2,0,1:T(4,128)(2,1)S(1)} all-gather(bf16[3,96,192]{2,0,1:T(4,128)(2,1)S(1)} %copy.261), channel_id=1, replica_groups=mesh['dp'=8,'mp'=4] {'dp'}, dimensions={1}, use_global_device_ids=true | all-gather | bytes 995328 | tf_op jit(solution)/shard_map/all_gather | solution.py:352
  827.0 2.2 copy.266
  829.2 204.6 %all-gather.11.cloned.1.call-done = bf16[8192,768]{1,0:T(8,128)(2,1)} async-done(((bf16[2048,768]{1,0:T(8,128)(2,1)}), bf16[8192,768]{1,0:T(8,128)(2,1)}) %all-gather.11.cloned.1.call-update) | async-done | bytes 12582928 | tf_op jit(solution)/shard_map/all_gather | solution.py:339
  1033.8 9.0 reduce_sum.525
  1042.8 6.3 add_convert_fusion
  (504 shorter events, 88.9 us)
Async XLA Ops:
  7.2 216.4 %copy-start = (bf16[768,768]{1,0:T(8,128)(2,1)S(1)}, bf16[768,768]{1,0:T(8,128)(2,1)}, u32[]{:S(2)}) copy-start(bf16[768,768]{1,0:T(8,128)(2,1)} %param.23) | copy-start | bytes 3538948
  7.2 209.8 %all-reduce.72.cloned.1.call-start = ((), (), s32[]{:S(2)}) async-start(), calls=%async_computation.6 | async-start | bytes 6291456 | tf_op jit(solution)/shard_map/psum | solution.py:288
  13.9 10.1 copy-start.96
  13.9 18.9 %copy-start.76 = (f32[64,64]{1,0:T(8,128)}, f32[64,64]{1,0:T(8,128)S(1)}, u32[]{:S(2)}) copy-start(f32[64,64]{1,0:T(8,128)S(1)} %fusion.106) | copy-start | bytes 49156
  13.9 20.8 %copy-start.28 = (f32[64,64]{1,0:T(8,128)}, f32[64,64]{1,0:T(8,128)S(1)}, u32[]{:S(2)}) copy-start(f32[64,64]{1,0:T(8,128)S(1)} %get-tuple-element.209) | copy-start | bytes 49156
  13.9 20.8 %copy-start.78 = (f32[64,64]{1,0:T(8,128)}, f32[64,64]{1,0:T(8,128)S(1)}, u32[]{:S(2)}) copy-start(f32[64,64]{1,0:T(8,128)S(1)} %get-tuple-element.210) | copy-start | bytes 49156
  25.2 18.8 %copy-start.100 = (f32[2,3,64]{2,1,0:T(4,128)}, f32[2,3,64]{2,1,0:T(4,128)S(1)}, u32[]{:S(2)}) copy-start(f32[2,3,64]{2,1,0:T(4,128)S(1)} %get-tuple-element.194) | copy-start | bytes 4612
  44.1 4.8 copy-start.73
  47.1 40.2 %copy-start.71 = (f32[2,3,64,64]{3,2,1,0:T(8,128)}, f32[2,3,64,64]{3,2,1,0:T(8,128)S(1)}, u32[]{:S(2)}) copy-start(f32[2,3,64,64]{3,2,1,0:T(8,128)S(1)} %fusion.45) | copy-start | bytes 294916
  93.1 274.2 %all-reduce.74.cloned.1.call-start = ((), (), s32[]{:S(2)}) async-start(), calls=%async_computation.7 | async-start | bytes 6291456 | tf_op jit(solution)/shard_map/psum | solution.py:298
  217.0 3.9 copy-start.11
  217.0 4.7 copy-start.13
  223.6 17.8 %copy-start.2 = (f32[2048,768]{1,0:T(8,128)}, f32[2048,768]{1,0:T(8,128)S(1)}, u32[]{:S(2)}) copy-start(f32[2048,768]{1,0:T(8,128)S(1)} %get-tuple-element.151) | copy-start | bytes 18874372
  223.6 19.5 %copy-start.153 = (bf16[768,768]{1,0:T(8,128)(2,1)S(1)}, bf16[768,768]{1,0:T(8,128)(2,1)}, u32[]{:S(2)}) copy-start(bf16[768,768]{1,0:T(8,128)(2,1)} %param.24) | copy-start | bytes 3538948
  247.1 266.4 %all-reduce.76.cloned.1.call-start = ((), (), s32[]{:S(2)}) async-start(), calls=%async_computation.8 | async-start | bytes 6291456 | tf_op jit(solution)/shard_map/psum | solution.py:317
  374.0 7.6 slice-start
  374.0 7.6 slice-start.2
  376.7 4.9 copy-start.154
  376.7 4.9 slice-start.1
  376.7 4.9 slice-start.3
  381.6 5.5 copy-start.3
  393.3 226.1 %reduce-scatter.17.cloned.1.call-start = ((), (), s32[]{:S(2)}) async-start(), calls=%async_computation.11 | async-start | bytes 2654208 | tf_op jit(solution)/shard_map/reduce_scatter | solution.py:348
  401.3 253.6 %reduce-scatter.15.cloned.1.call-start = ((), (), s32[]{:S(2)}) async-start(), calls=%async_computation.9 | async-start | bytes 2654208 | tf_op jit(solution)/shard_map/reduce_scatter | solution.py:347
  401.5 5.1 copy-start.156
  413.6 284.0 %reduce-scatter.23.cloned.1.call-start = ((), (), s32[]{:S(2)}) async-start(), calls=%async_computation.16 | async-start | bytes 442368
  513.5 7.6 copy-start.10
  521.1 8.8 copy-start.81
  566.3 7.8 copy-start.8
  566.3 7.8 copy-start.147
  574.1 9.1 copy-start.62
  591.3 5.6 copy-start.85
  591.3 5.6 copy-start.110
  591.3 5.6 copy-start.151
  596.8 5.6 copy-start.95
  596.8 5.6 copy-start.97
  596.8 111.4 %reduce-scatter.25.cloned.1.call-start = ((), (), s32[]{:S(2)}) async-start(), calls=%async_computation.17 | async-start | bytes 442368
  602.4 116.2 %reduce-scatter.21.cloned.1.call-start = ((), (), s32[]{:S(2)}) async-start(), calls=%async_computation.15 | async-start | bytes 884736
  605.3 138.6 %all-gather.9.cloned.1.call-start = ((), (), s32[]{:S(2)}) async-start(), calls=%async_computation.12 | async-start | bytes 1327104 | tf_op jit(solution)/shard_map/all_gather | solution.py:364
  610.5 10.9 %copy-start.83 = (bf16[2,64,3,64]{3,1,2,0:T(8,128)(2,1)S(1)}, bf16[2,64,3,64]{3,1,2,0:T(8,128)(2,1)}, u32[]{:S(2)}) copy-start(bf16[2,64,3,64]{3,1,2,0:T(8,128)(2,1)} %copy-done.82) | copy-start | bytes 147460
  610.5 10.9 %copy-start.111 = (f32[2,3,64]{2,1,0:T(4,128)S(1)}, f32[2,3,64]{2,1,0:T(4,128)}, u32[]{:S(2)}) copy-start(f32[2,3,64]{2,1,0:T(4,128)} %neg.102) | copy-start | bytes 4612
  610.5 10.9 %copy-start.152 = (f32[2,64]{1,0:T(2,128)S(1)}, f32[2,64]{1,0:T(2,128)}, u32[]{:S(2)}) copy-start(f32[2,64]{1,0:T(2,128)} %copy-done.150) | copy-start | bytes 1540
  619.1 5.3 copy-start.130
  619.1 5.3 copy-start.131
  619.2 5.3 copy-start.132
  619.2 5.3 copy-start.133
  619.2 5.3 copy-start.134
  619.2 5.3 copy-start.135
  619.2 5.3 copy-start.136
  619.2 5.3 copy-start.137
  619.2 5.3 copy-start.138
  619.2 5.3 copy-start.139
  619.2 5.3 copy-start.140
  619.2 5.3 copy-start.141
  619.2 5.3 copy-start.142
  619.3 5.3 copy-start.143
  619.3 5.3 copy-start.144
  619.3 5.3 copy-start.145
  619.3 5.3 copy-start.146
  621.0 148.7 %all-gather.7.cloned.1.call-start = ((), (), s32[]{:S(2)}) async-start(), calls=%async_computation.10 | async-start | bytes 1327104 | tf_op jit(solution)/shard_map/all_gather | solution.py:361
  656.5 157.0 %reduce-scatter.19.cloned.1.call-start = ((), (), s32[]{:S(2)}) async-start(), calls=%async_computation.14 | async-start | bytes 2211840
  665.1 4.9 copy-start.26
  665.1 4.9 copy-start.87
  690.4 343.4 %all-gather.11.cloned.1.call-start = ((), (), s32[]{:S(2)}) async-start(), calls=%async_computation.13 | async-start | bytes 15728640 | tf_op jit(solution)/shard_map/all_gather | solution.py:339
  1042.8 6.3 copy-start.1
  (110 other events, 195.1 us)
Sparse Core Ops, SparseCore 0:
  93.2 123.7 all-reduce.71
  247.2 120.0 all-reduce.73
  393.4 120.0 all-reduce.75
  517.3 41.5 reduce-scatter.16
  563.0 42.4 reduce-scatter.14
  609.0 33.7 reduce-scatter.22
  645.9 33.8 reduce-scatter.24
  682.9 34.9 reduce-scatter.20
  719.8 24.0 all-gather.8
  745.6 24.0 all-gather.6
  773.1 40.3 reduce-scatter.18
  815.5 218.1 all-gather.10
